TPU v7x, 32 devices: a whole 2x2x4 slice. The times are simulated.
32 devices in a mesh: day: 2 (over y), stu: 16 (over z, x, core).
Axes of the slice: x: 2, y: 2, z: 4, core: 2. Of those that a mesh axis runs over, the one named last changes fastest.
Arguments:
- performance: bfloat16 [64, 128, 1024], P('day', 'stu'), may hold values from -8 to 8
- student_factor: bfloat16 [128, 256], P('stu'), may hold values from -0.5 to 0.5
- skill_factor: bfloat16 [1024, 256], replicated, may hold values from -0.1875 to 0.1875
- day_prev: float32 [64, 256], P('day'), may hold values from -6 to 6
- ar_coef: float32 [7], replicated, may hold values from -0.3 to 0.3
Outputs:
- day_factor: float32 [64, 256], P('day', 'stu')
- residual: float32 [64, 256], P('day', 'stu')
All inputs are finite; a program needn't handle non-finite values.
Results may differ from a plain program's by a relative error of at most 0.0003.
Values sent between devices are 32-bit elements; how exact they have to be, the bound alone decides.
No kernel may reach another device: no remote copies, remote signals or barrier semaphores. Data moves between devices by JAX's collectives and lax.ppermute only.
A program may use at most 64 MiB of HBM per device.

v0:
```python
import jax
import jax.numpy as jnp
from jax import lax
from jax.sharding import PartitionSpec as P

LAGS = 7
ITERS = 3
smoothing = 1.0


def shifted(block, axis, distance):
    devices = range(lax.axis_size(axis))
    route = [(i - distance, i) for i in devices if i - distance in devices]
    return lax.ppermute(block, axis, route)


def filter_rows(extended, coef, count):
    out = extended[LAGS : LAGS + count]
    for lag in range(1, LAGS + 1):
        out = out - coef[lag - 1] * extended[LAGS - lag : LAGS - lag + count]
    return out


def smooth(values, coef):
    count = values.shape[0]
    below = shifted(values[count - LAGS :], "day", 1)
    ahead_core = filter_rows(jnp.concatenate([below, values], 0), coef, count)
    above = shifted(ahead_core[:LAGS], "day", -1)
    ahead = jnp.concatenate([ahead_core, above], 0)
    out = ahead[:count]
    for lag in range(1, LAGS + 1):
        out = out - coef[lag - 1] * ahead[lag : lag + count]
    return out


def with_gram(values, gram_part):
    return jnp.dot(
        lax.all_gather(values, "stu", axis=1, tiled=True),
        gram_part,
        precision=lax.Precision.HIGHEST,
        preferred_element_type=jnp.float32,
    )


def operate(values, gram_part, coef):
    return with_gram(values, gram_part) + smoothing * smooth(values, coef)


def global_total(value):
    return lax.psum(value, ("day", "stu"))


def summed_gram(local_gram):
    return lax.psum(local_gram, "stu")


def local(performance, student_factor, skill_factor, day_prev, ar_coef):
    days, students, skills = performance.shape
    rank = skill_factor.shape[1]
    proj = jnp.dot(
        performance.reshape(days * students, skills),
        skill_factor,
        preferred_element_type=jnp.float32,
    )
    proj = proj.reshape(days, students, rank)
    local_terms = jnp.sum(proj * student_factor.astype(jnp.float32)[None], axis=1)
    local_gram = jnp.dot(student_factor.T, student_factor, preferred_element_type=jnp.float32)
    skill_gram = jnp.dot(skill_factor.T, skill_factor, preferred_element_type=jnp.float32)
    columns = rank // lax.axis_size("stu")
    first_col = lax.axis_index("stu") * columns
    gram = summed_gram(local_gram) * skill_gram
    mttkrp = lax.psum_scatter(local_terms, "stu", scatter_dimension=1, tiled=True)
    gram_part = lax.dynamic_slice_in_dim(gram, first_col, columns, 1)
    day_factor = lax.dynamic_slice_in_dim(day_prev, first_col, columns, 1)
    residual = mttkrp - operate(day_factor, gram_part, ar_coef)
    direction = residual
    norm_now = global_total(jnp.sum(residual * residual))
    for step in range(ITERS):
        image = operate(direction, gram_part, ar_coef)
        alpha = norm_now / global_total(jnp.sum(direction * image))
        day_factor = day_factor + alpha * direction
        residual = residual - alpha * image
        norm_next = global_total(jnp.sum(residual * residual))
        direction = residual + norm_next / norm_now * direction
        norm_now = norm_next
    return (day_factor, residual)


def solution(mesh):
    return jax.shard_map(
        local,
        mesh=mesh,
        in_specs=(P("day", "stu", None), P("stu", None), P(), P("day", None), P()),
        out_specs=(P("day", "stu"), P("day", "stu")),
        check_vma=False,
    )
```

profile of v0, /device:TPU:14, one launch (start us, length us, event | category | flops | bytes accessed | tf_op | source)
XLA Modules:
  0.0 491.8 jit_solution(908321572501885240)
XLA Ops:
  7.2 0.0 copy-start
  7.2 0.0 copy-start.1
  7.2 0.0 all-reduce.3.cloned.1.call-start
  7.2 0.9 constant_dynamic-slice_fusion
  8.1 0.1 copy.10
  8.2 0.1 slice.333
  8.3 1.3 collective-permute-start
  9.6 1.7 fusion.139
  11.2 0.0 copy-start.2
  11.2 0.0 all-reduce.3.cloned.1.call-update
  11.3 0.0 reduce-scatter.2.cloned.1.call-start
  11.3 0.6 copy-done.2
  11.9 0.0 copy-done
  11.9 0.0 copy-done.1
  11.9 0.3 fusion
  12.3 0.8 copy.9
  13.0 0.0 reduce-scatter.2.cloned.1.call-update
  13.0 0.0 copy-start.3
  13.1 0.3 fusion.140
  13.4 0.3 copy-done.3
  13.7 0.7 fusion.138
  14.3 15.5 %all_gather.12 = f32[32,256]{0,1:T(8,128)S(1)} all-gather(f32[32,16]{0,1:T(8,128)S(1)} %copy.10), channel_id=1, replica_groups=mesh['day'=2,'stu'=16] {'stu'}, dimensions={1}, use_global_device_ids=true | all-gather | bytes 34816 | tf_op jit(solution)/shard_map/all_gather | solution.py:38
  29.8 0.0 collective-permute-done
  29.8 4.5 fusion.120
  34.3 4.6 collective-permute-start.1
  38.9 64.2 %all-reduce.3.cloned.1.call-done = f32[256,256]{0,1:T(8,128)} async-done(((f32[256,256]{0,1:T(8,128)}), f32[256,256]{0,1:T(8,128)}) %all-reduce.3.cloned.1.call-update) | async-done | bytes 262160 | tf_op jit(solution)/shard_map/psum | solution.py:54
  103.1 0.7 dynamic-slice_multiply_fusion
  103.8 0.0 collective-permute-done.1
  103.8 57.7 %reduce-scatter.2.cloned.1.call-done = f32[32,16]{0,1:T(8,128)} async-done(((f32[32,256]{0,1:T(8,128)}), f32[32,16]{0,1:T(8,128)}) %reduce-scatter.2.cloned.1.call-update) | async-done | bytes 2064 | tf_op jit(solution)/shard_map/reduce_scatter | solution.py:72
  161.5 5.2 %fusion.104 = f32[32,16]{0,1:T(8,128)S(1)} fusion(f32[32,16]{0,1:T(8,128)} %reduce-scatter.2.cloned.1.call-done, f32[7,16]{0,1:T(8,128)S(1)} %collective-permute-done.1, f32[32,16]{0,1:T(8,128)S(1)} %fusion.120, f32[]{:T(128)} %bitcast.7, f32[]{:T(128)} %bitcast.6, f32[]{:T(128)} %bitcast.5, f32[]{:T(128)} %bitcast.4, f32[]{:T(128)} %bitcast.3, ...), kind=kOutput, calls=%fused_computation.173 | convolution fusion | flops 1584640 | bytes 55772 | tf_op jit(solution)/shard_map/dot_general | solution.py:37
  166.7 0.1 slice.359
  166.8 1.3 collective-permute-start.2
  168.1 4.2 collective-permute-done.2
  172.3 4.5 fusion.86
  176.8 1.6 collective-permute-start.3
  178.5 15.4 %all_gather.13 = f32[32,256]{0,1:T(8,128)S(1)} all-gather(f32[32,16]{0,1:T(8,128)S(1)} %fusion.104), channel_id=1, replica_groups=mesh['day'=2,'stu'=16] {'stu'}, dimensions={1}, use_global_device_ids=true | all-gather | bytes 34816 | tf_op jit(solution)/shard_map/all_gather | solution.py:38
  193.8 0.0 collective-permute-done.3
  193.8 5.2 %multiply_reduce_fusion.4 = (f32[]{:T(128)}, f32[]{:T(128)}, f32[32,16]{0,1:T(8,128)S(1)}) fusion(f32[32,16]{0,1:T(8,128)S(1)} %fusion.104, f32[7,16]{0,1:T(8,128)S(1)} %collective-permute-done.3, f32[32,16]{0,1:T(8,128)S(1)} %fusion.86, f32[]{:T(128)} %bitcast.7, f32[]{:T(128)} %bitcast.6, f32[]{:T(128)} %bitcast.5, f32[]{:T(128)} %bitcast.4, ...), kind=kOutput, calls=%fused_computation.235 | convolution fusion | flops 1586174 | bytes 55780 | tf_op jit(solution)/shard_map/dot_general | solution.py:37
  199.0 44.1 %all-reduce = (f32[]{:T(128)}, f32[]{:T(128)}) all-reduce(f32[]{:T(128)} %get-tuple-element.3, f32[]{:T(128)} %get-tuple-element.2), channel_id=1, replica_groups=mesh['day'=2,'stu'=16] {'day','stu'}, use_global_device_ids=true, to_apply=%region_4.0 | all-reduce | flops 2 | bytes 16 | tf_op jit(solution)/shard_map/psum | solution.py:50
  244.4 0.6 multiply_reduce_fusion.3
  245.1 38.6 %psum.52 = f32[]{:T(128)} all-reduce(f32[]{:T(128)} %multiply_reduce_fusion.3), channel_id=1, replica_groups=mesh['day'=2,'stu'=16] {'day','stu'}, use_global_device_ids=true, to_apply=%region_8.0 | all-reduce | flops 1 | bytes 8 | tf_op jit(solution)/shard_map/psum | solution.py:50
  285.1 0.1 slice.385
  285.1 1.3 collective-permute-start.4
  286.4 4.2 collective-permute-done.4
  290.7 4.5 fusion.53
  295.1 1.6 collective-permute-start.5
  296.8 18.0 %all_gather.14 = f32[32,256]{0,1:T(8,128)S(1)} all-gather(f32[32,16]{0,1:T(8,128)S(1)} %multiply_add_fusion.2), channel_id=1, replica_groups=mesh['day'=2,'stu'=16] {'stu'}, dimensions={1}, use_global_device_ids=true | all-gather | bytes 34816 | tf_op jit(solution)/shard_map/all_gather | solution.py:38
  314.8 0.0 collective-permute-done.5
  314.8 5.2 %multiply_reduce_fusion.2 = (f32[]{:T(128)}, f32[32,16]{0,1:T(8,128)S(1)}) fusion(f32[32,16]{0,1:T(8,128)S(1)} %multiply_add_fusion.2, f32[7,16]{0,1:T(8,128)S(1)} %collective-permute-done.5, f32[32,16]{0,1:T(8,128)S(1)} %fusion.53, f32[]{:T(128)} %bitcast.7, f32[]{:T(128)} %bitcast.6, f32[]{:T(128)} %bitcast.5, f32[]{:T(128)} %bitcast.4, f32[]{:T(128)} %bitcast.3, ...), kind=kOutput, calls=%fused_computation.231 | convolution fusion | flops 1585151 | bytes 55776 | tf_op jit(solution)/shard_map/dot_general | solution.py:37
  320.0 43.0 %psum.53 = f32[]{:T(128)} all-reduce(f32[]{:T(128)} %get-tuple-element.10), channel_id=1, replica_groups=mesh['day'=2,'stu'=16] {'day','stu'}, use_global_device_ids=true, to_apply=%region_10.0 | all-reduce | flops 1 | bytes 8 | tf_op jit(solution)/shard_map/psum | solution.py:50
  364.2 0.6 multiply_reduce_fusion.1
  364.8 39.0 %psum.54 = f32[]{:T(128)} all-reduce(f32[]{:T(128)} %get-tuple-element.8), channel_id=1, replica_groups=mesh['day'=2,'stu'=16] {'day','stu'}, use_global_device_ids=true, to_apply=%region_12.0 | all-reduce | flops 1 | bytes 8 | tf_op jit(solution)/shard_map/psum | solution.py:50
  405.2 0.1 slice.411
  405.3 1.3 collective-permute-start.6
  406.5 4.2 collective-permute-done.6
  410.8 4.5 fusion.20
  415.3 1.6 collective-permute-start.7
  416.9 17.6 %all_gather.15 = f32[32,256]{0,1:T(8,128)S(1)} all-gather(f32[32,16]{0,1:T(8,128)S(1)} %multiply_add_fusion.1), channel_id=1, replica_groups=mesh['day'=2,'stu'=16] {'stu'}, dimensions={1}, use_global_device_ids=true | all-gather | bytes 34816 | tf_op jit(solution)/shard_map/all_gather | solution.py:38
  434.5 0.0 collective-permute-done.7
  434.5 5.1 %multiply_reduce_fusion = (f32[]{:T(128)}, f32[32,16]{0,1:T(8,128)S(1)}) fusion(f32[32,16]{0,1:T(8,128)S(1)} %multiply_add_fusion.1, f32[7,16]{0,1:T(8,128)S(1)} %collective-permute-done.7, f32[32,16]{0,1:T(8,128)S(1)} %fusion.20, f32[]{:T(128)} %bitcast.7, f32[]{:T(128)} %bitcast.6, f32[]{:T(128)} %bitcast.5, f32[]{:T(128)} %bitcast.4, f32[]{:T(128)} %bitcast.3, ...), kind=kOutput, calls=%fused_computation.227 | convolution fusion | flops 1585151 | bytes 55776 | tf_op jit(solution)/shard_map/dot_general | solution.py:37
  439.7 43.2 %psum.55 = f32[]{:T(128)} all-reduce(f32[]{:T(128)} %get-tuple-element.6), channel_id=1, replica_groups=mesh['day'=2,'stu'=16] {'day','stu'}, use_global_device_ids=true, to_apply=%region_14.0 | all-reduce | flops 1 | bytes 8 | tf_op jit(solution)/shard_map/psum | solution.py:50
  484.3 0.6 multiply_subtract_fusion
  (3 shorter events, 0.0 us)
Async XLA Ops:
  7.2 4.8 copy-start
  7.2 4.8 copy-start.1
  7.2 95.9 %all-reduce.3.cloned.1.call-start = ((), (), s32[]{:S(2)}) async-start(), calls=%async_computation.2 | async-start | bytes 524288 | tf_op jit(solution)/shard_map/psum | solution.py:54
  8.3 21.6 %collective-permute-start = (f32[7,16]{0,1:T(8,128)S(1)}, f32[7,16]{0,1:T(8,128)S(1)}, u32[]{:S(2)}, u32[]{:S(2)}) collective-permute-start(f32[7,16]{0,1:T(8,128)S(1)} %slice.333), channel_id=1, source_target_pairs={{0,16},{1,17},{2,18},{3,19},{4,20},{5,21},{6,22},{7,23},{8,24},{9,... | collective-permute-start | bytes 1352 | tf_op jit(solution)/shard_map/ppermute | solution.py:14
  11.2 0.7 copy-start.2
  11.3 150.2 %reduce-scatter.2.cloned.1.call-start = ((), (), s32[]{:S(2)}) async-start(), calls=%async_computation.1 | async-start | bytes 139264 | tf_op jit(solution)/shard_map/reduce_scatter | solution.py:72
  13.0 0.7 copy-start.3
  34.3 69.5 %collective-permute-start.1 = (f32[7,16]{0,1:T(8,128)S(1)}, f32[7,16]{0,1:T(8,128)S(1)}, u32[]{:S(2)}, u32[]{:S(2)}) collective-permute-start(f32[7,16]{0,1:T(8,128)S(1)} %bitcast.27), channel_id=1, source_target_pairs={{16,0},{17,1},{18,2},{19,3},{20,4},{21,5},{22,6},{23,7},{24,8},{25... | collective-permute-start | bytes 1352 | tf_op jit(solution)/shard_map/ppermute | solution.py:14
  166.8 5.5 %collective-permute-start.2 = (f32[7,16]{0,1:T(8,128)S(1)}, f32[7,16]{0,1:T(8,128)S(1)}, u32[]{:S(2)}, u32[]{:S(2)}) collective-permute-start(f32[7,16]{0,1:T(8,128)S(1)} %slice.359), channel_id=1, source_target_pairs={{0,16},{1,17},{2,18},{3,19},{4,20},{5,21},{6,22},{7,23},{8,24},{9,... | collective-permute-start | bytes 1352 | tf_op jit(solution)/shard_map/ppermute | solution.py:14
  176.8 17.0 %collective-permute-start.3 = (f32[7,16]{0,1:T(8,128)S(1)}, f32[7,16]{0,1:T(8,128)S(1)}, u32[]{:S(2)}, u32[]{:S(2)}) collective-permute-start(f32[7,16]{0,1:T(8,128)S(1)} %bitcast.29), channel_id=1, source_target_pairs={{16,0},{17,1},{18,2},{19,3},{20,4},{21,5},{22,6},{23,7},{24,8},{25... | collective-permute-start | bytes 1352 | tf_op jit(solution)/shard_map/ppermute | solution.py:14
  285.1 5.5 %collective-permute-start.4 = (f32[7,16]{0,1:T(8,128)S(1)}, f32[7,16]{0,1:T(8,128)S(1)}, u32[]{:S(2)}, u32[]{:S(2)}) collective-permute-start(f32[7,16]{0,1:T(8,128)S(1)} %slice.385), channel_id=1, source_target_pairs={{0,16},{1,17},{2,18},{3,19},{4,20},{5,21},{6,22},{7,23},{8,24},{9,... | collective-permute-start | bytes 1352 | tf_op jit(solution)/shard_map/ppermute | solution.py:14
  295.1 19.6 %collective-permute-start.5 = (f32[7,16]{0,1:T(8,128)S(1)}, f32[7,16]{0,1:T(8,128)S(1)}, u32[]{:S(2)}, u32[]{:S(2)}) collective-permute-start(f32[7,16]{0,1:T(8,128)S(1)} %bitcast.30), channel_id=1, source_target_pairs={{16,0},{17,1},{18,2},{19,3},{20,4},{21,5},{22,6},{23,7},{24,8},{25... | collective-permute-start | bytes 1352 | tf_op jit(solution)/shard_map/ppermute | solution.py:14
  405.3 5.5 %collective-permute-start.6 = (f32[7,16]{0,1:T(8,128)S(1)}, f32[7,16]{0,1:T(8,128)S(1)}, u32[]{:S(2)}, u32[]{:S(2)}) collective-permute-start(f32[7,16]{0,1:T(8,128)S(1)} %slice.411), channel_id=1, source_target_pairs={{0,16},{1,17},{2,18},{3,19},{4,20},{5,21},{6,22},{7,23},{8,24},{9,... | collective-permute-start | bytes 1352 | tf_op jit(solution)/shard_map/ppermute | solution.py:14
  415.3 19.3 %collective-permute-start.7 = (f32[7,16]{0,1:T(8,128)S(1)}, f32[7,16]{0,1:T(8,128)S(1)}, u32[]{:S(2)}, u32[]{:S(2)}) collective-permute-start(f32[7,16]{0,1:T(8,128)S(1)} %bitcast.28), channel_id=1, source_target_pairs={{16,0},{17,1},{18,2},{19,3},{20,4},{21,5},{22,6},{23,7},{24,8},{25... | collective-permute-start | bytes 1352 | tf_op jit(solution)/shard_map/ppermute | solution.py:14
Sparse Core Ops, SparseCore 0:
  11.4 91.6 all-reduce.2
  106.5 54.8 reduce-scatter.1
where the time goes:
time: 494 us; the launch traced here: 492 us
  blocking collectives  274 us (55%)
  waiting for transfers between devices  135 us (27%)
  matrix products  23.1 us (5%)
  between operations  20.9 us (4%)
  other arithmetic  20.4 us (4%)
  starting transfers between devices  14.7 us (3%)
    psum x5, blocking collectives, global_total(): return lax.psum(value, ('day', 'stu'))  208 us
    all_gather x4, blocking collectives, with_gram(): lax.all_gather(values, 'stu', axis=1, tiled=True)  66.5 us
    psum x1, waiting for transfers between devices, summed_gram(): return lax.psum(local_gram, 'stu')  64.2 us
    reduce_scatter x1, waiting for transfers between devices, local(): lax.psum_scatter(local_terms, 'stu', scatter_dimension=1, tiled=True)  57.7 us
    dot_general x4, matrix products, with_gram(): jnp.dot(lax.all_gather(values, 'stu', axis=1, tiled=True), gram_part, pre...  20.8 us
    sub x4, other arithmetic, filter_rows(): out = out - coef[lag - 1] * extended[LAGS - lag:LAGS - lag + count]  17.8 us
    ppermute x8, starting transfers between devices, shifted(): return lax.ppermute(block, axis, route)  14.6 us
    ppermute x8, waiting for transfers between devices, shifted(): return lax.ppermute(block, axis, route)  12.7 us
  transfers between devices with their start and end apart: 10, of which 5 were waited for; matrix products, arithmetic and copies ran while one was open for 2% of the time, Pallas kernels for 0%

commit v1 on v0

--- a/solution.py
+++ b/solution.py
@@ -47,7 +47,7 @@
 
 
 def global_total(value):
-    return lax.psum(value, ("day", "stu"))
+    return lax.psum(lax.psum(value, "stu"), "day")
 
 
 def summed_gram(local_gram):

time: 494 us -> 473 us (0.957)
  the two profiles are of different devices: /device:TPU:14 before, /device:TPU:0 now
where the time goes in v1:
time: 473 us; the launch traced here: 471 us
  blocking collectives  261 us (55%)
  waiting for transfers between devices  121 us (26%)
  matrix products  23.3 us (5%)
  starting transfers between devices  21.4 us (5%)
  between operations  20.7 us (4%)
  other arithmetic  20.5 us (4%)
    psum x10, blocking collectives, global_total(): return lax.psum(lax.psum(value, 'stu'), 'day')  184 us
    all_gather x4, blocking collectives, with_gram(): lax.all_gather(values, 'stu', axis=1, tiled=True)  76.7 us
    psum x1, waiting for transfers between devices, summed_gram(): return lax.psum(local_gram, 'stu')  58.5 us
    reduce_scatter x1, waiting for transfers between devices, local(): lax.psum_scatter(local_terms, 'stu', scatter_dimension=1, tiled=True)  58.3 us
    ppermute x8, starting transfers between devices, shifted(): return lax.ppermute(block, axis, route)  21.3 us
    dot_general x4, matrix products, with_gram(): jnp.dot(lax.all_gather(values, 'stu', axis=1, tiled=True), gram_part, pre...  20.9 us
    sub x4, other arithmetic, filter_rows(): out = out - coef[lag - 1] * extended[LAGS - lag:LAGS - lag + count]  17.8 us
  transfers between devices with their start and end apart: 10, of which 5 were waited for; matrix products, arithmetic and copies ran while one was open for 2% of the time, Pallas kernels for 0%

profile of v1, /device:TPU:0, one launch (start us, length us, event | category | flops | bytes accessed | tf_op | source)
XLA Modules:
  0.0 471.4 jit_solution(8854464314555483708)
XLA Ops:
  7.2 0.0 copy-start
  7.2 0.0 copy-start.1
  7.2 0.0 all-reduce.4.cloned.1.call-start
  7.2 0.9 constant_dynamic-slice_fusion
  8.1 0.1 copy.10
  8.2 0.1 slice.333
  8.3 4.9 %collective-permute-start = (f32[7,16]{0,1:T(8,128)S(1)}, f32[7,16]{0,1:T(8,128)S(1)}, u32[]{:S(2)}, u32[]{:S(2)}) collective-permute-start(f32[7,16]{0,1:T(8,128)S(1)} %slice.333), channel_id=1, source_target_pairs={{0,16},{1,17},{2,18},{3,19},{4,20},{5,21},{6,22},{7,23},{8,24},{9,... | collective-permute-start | bytes 1352 | tf_op jit(solution)/shard_map/ppermute | solution.py:14
  13.1 1.7 fusion.139
  14.8 0.0 all-reduce.4.cloned.1.call-update
  14.8 0.0 reduce-scatter.2.cloned.1.call-start
  14.9 0.6 copy-done.2
  15.5 0.3 fusion
  15.8 0.8 copy.9
  16.6 0.0 reduce-scatter.2.cloned.1.call-update
  16.6 0.0 copy-start.3
  16.6 0.3 fusion.140
  17.0 0.3 copy-done.3
  17.3 0.7 fusion.138
  17.9 22.0 %all_gather.12 = f32[32,256]{0,1:T(8,128)S(1)} all-gather(f32[32,16]{0,1:T(8,128)S(1)} %copy.10), channel_id=1, replica_groups=mesh['day'=2,'stu'=16] {'stu'}, dimensions={1}, use_global_device_ids=true | all-gather | bytes 34816 | tf_op jit(solution)/shard_map/all_gather | solution.py:38
  39.9 0.0 collective-permute-done
  39.9 4.5 fusion.120
  44.4 1.3 collective-permute-start.1
  45.7 58.5 %all-reduce.4.cloned.1.call-done = f32[256,256]{0,1:T(8,128)} async-done(((f32[256,256]{0,1:T(8,128)}), f32[256,256]{0,1:T(8,128)}) %all-reduce.4.cloned.1.call-update) | async-done | bytes 262160 | tf_op jit(solution)/shard_map/psum | solution.py:54
  104.1 0.7 dynamic-slice_multiply_fusion
  104.9 0.0 collective-permute-done.1
  104.9 58.3 %reduce-scatter.2.cloned.1.call-done = f32[32,16]{0,1:T(8,128)} async-done(((f32[32,256]{0,1:T(8,128)}), f32[32,16]{0,1:T(8,128)}) %reduce-scatter.2.cloned.1.call-update) | async-done | bytes 2064 | tf_op jit(solution)/shard_map/reduce_scatter | solution.py:72
  163.2 5.2 %fusion.104 = f32[32,16]{0,1:T(8,128)S(1)} fusion(f32[32,16]{0,1:T(8,128)} %reduce-scatter.2.cloned.1.call-done, f32[7,16]{0,1:T(8,128)S(1)} %collective-permute-done.1, f32[32,16]{0,1:T(8,128)S(1)} %fusion.120, f32[]{:T(128)} %bitcast.7, f32[]{:T(128)} %bitcast.6, f32[]{:T(128)} %bitcast.5, f32[]{:T(128)} %bitcast.4, f32[]{:T(128)} %bitcast.3, ...), kind=kOutput, calls=%fused_computation.173 | convolution fusion | flops 1584640 | bytes 55772 | tf_op jit(solution)/shard_map/dot_general | solution.py:37
  168.4 0.1 slice.359
  168.5 3.4 collective-permute-start.2
  171.9 1.3 collective-permute-done.2
  173.2 4.5 fusion.86
  177.7 1.3 collective-permute-start.3
  179.0 19.8 %all_gather.13 = f32[32,256]{0,1:T(8,128)S(1)} all-gather(f32[32,16]{0,1:T(8,128)S(1)} %fusion.104), channel_id=1, replica_groups=mesh['day'=2,'stu'=16] {'stu'}, dimensions={1}, use_global_device_ids=true | all-gather | bytes 34816 | tf_op jit(solution)/shard_map/all_gather | solution.py:38
  198.8 0.0 collective-permute-done.3
  198.8 5.2 %multiply_reduce_fusion.4 = (f32[]{:T(128)}, f32[]{:T(128)}, f32[32,16]{0,1:T(8,128)S(1)}) fusion(f32[32,16]{0,1:T(8,128)S(1)} %fusion.104, f32[7,16]{0,1:T(8,128)S(1)} %collective-permute-done.3, f32[32,16]{0,1:T(8,128)S(1)} %fusion.86, f32[]{:T(128)} %bitcast.7, f32[]{:T(128)} %bitcast.6, f32[]{:T(128)} %bitcast.5, f32[]{:T(128)} %bitcast.4, ...), kind=kOutput, calls=%fused_computation.235 | convolution fusion | flops 1586174 | bytes 55780 | tf_op jit(solution)/shard_map/dot_general | solution.py:37
  204.0 30.5 %all-reduce = (f32[]{:T(128)}, f32[]{:T(128)}) all-reduce(f32[]{:T(128)} %get-tuple-element.3, f32[]{:T(128)} %get-tuple-element.2), channel_id=1, replica_groups=mesh['day'=2,'stu'=16] {'stu'}, use_global_device_ids=true, to_apply=%region_4.0 | all-reduce | flops 2 | bytes 16 | tf_op jit(solution)/shard_map/psum | solution.py:50
  234.5 6.2 %all-reduce.1 = (f32[]{:T(128)}, f32[]{:T(128)}) all-reduce(f32[]{:T(128)} %get-tuple-element.4, f32[]{:T(128)} %get-tuple-element.5), channel_id=1, replica_groups=mesh['day'=2,'stu'=16] {'day'}, use_global_device_ids=true, to_apply=%region_5.0 | all-reduce | flops 2 | bytes 16 | tf_op jit(solution)/shard_map/psum | solution.py:50
  242.1 0.6 multiply_reduce_fusion.3
  242.7 30.1 %psum.96 = f32[]{:T(128)} all-reduce(f32[]{:T(128)} %multiply_reduce_fusion.3), channel_id=1, replica_groups=mesh['day'=2,'stu'=16] {'stu'}, use_global_device_ids=true, to_apply=%region_10.0 | all-reduce | flops 1 | bytes 8 | tf_op jit(solution)/shard_map/psum | solution.py:50
  272.9 5.6 %psum.97 = f32[]{:T(128)} all-reduce(f32[]{:T(128)} %psum.96), channel_id=1, replica_groups=mesh['day'=2,'stu'=16] {'day'}, use_global_device_ids=true, to_apply=%region_11.0 | all-reduce | flops 1 | bytes 8 | tf_op jit(solution)/shard_map/psum | solution.py:50
  279.8 0.1 slice.385
  279.9 3.9 collective-permute-start.4
  283.8 1.3 collective-permute-done.4
  285.2 4.5 fusion.53
  289.7 1.3 collective-permute-start.5
  291.0 17.5 %all_gather.14 = f32[32,256]{0,1:T(8,128)S(1)} all-gather(f32[32,16]{0,1:T(8,128)S(1)} %multiply_add_fusion.2), channel_id=1, replica_groups=mesh['day'=2,'stu'=16] {'stu'}, dimensions={1}, use_global_device_ids=true | all-gather | bytes 34816 | tf_op jit(solution)/shard_map/all_gather | solution.py:38
  308.4 0.0 collective-permute-done.5
  308.4 5.2 %multiply_reduce_fusion.2 = (f32[]{:T(128)}, f32[32,16]{0,1:T(8,128)S(1)}) fusion(f32[32,16]{0,1:T(8,128)S(1)} %multiply_add_fusion.2, f32[7,16]{0,1:T(8,128)S(1)} %collective-permute-done.5, f32[32,16]{0,1:T(8,128)S(1)} %fusion.53, f32[]{:T(128)} %bitcast.7, f32[]{:T(128)} %bitcast.6, f32[]{:T(128)} %bitcast.5, f32[]{:T(128)} %bitcast.4, f32[]{:T(128)} %bitcast.3, ...), kind=kOutput, calls=%fused_computation.231 | convolution fusion | flops 1585151 | bytes 55776 | tf_op jit(solution)/shard_map/dot_general | solution.py:37
  313.7 32.0 %psum.98 = f32[]{:T(128)} all-reduce(f32[]{:T(128)} %get-tuple-element.12), channel_id=1, replica_groups=mesh['day'=2,'stu'=16] {'stu'}, use_global_device_ids=true, to_apply=%region_13.0 | all-reduce | flops 1 | bytes 8 | tf_op jit(solution)/shard_map/psum | solution.py:50
  345.7 6.1 %psum.99 = f32[]{:T(128)} all-reduce(f32[]{:T(128)} %psum.98), channel_id=1, replica_groups=mesh['day'=2,'stu'=16] {'day'}, use_global_device_ids=true, to_apply=%region_14.0 | all-reduce | flops 1 | bytes 8 | tf_op jit(solution)/shard_map/psum | solution.py:50
  353.1 0.7 multiply_reduce_fusion.1
  353.8 30.1 %psum.100 = f32[]{:T(128)} all-reduce(f32[]{:T(128)} %get-tuple-element.10), channel_id=1, replica_groups=mesh['day'=2,'stu'=16] {'stu'}, use_global_device_ids=true, to_apply=%region_16.0 | all-reduce | flops 1 | bytes 8 | tf_op jit(solution)/shard_map/psum | solution.py:50
  383.9 5.6 %psum.101 = f32[]{:T(128)} all-reduce(f32[]{:T(128)} %psum.100), channel_id=1, replica_groups=mesh['day'=2,'stu'=16] {'day'}, use_global_device_ids=true, to_apply=%region_17.0 | all-reduce | flops 1 | bytes 8 | tf_op jit(solution)/shard_map/psum | solution.py:50
  390.7 0.1 slice.411
  390.7 3.9 collective-permute-start.6
  394.7 1.3 collective-permute-done.6
  396.0 4.5 fusion.20
  400.5 1.3 collective-permute-start.7
  401.8 17.5 %all_gather.15 = f32[32,256]{0,1:T(8,128)S(1)} all-gather(f32[32,16]{0,1:T(8,128)S(1)} %multiply_add_fusion.1), channel_id=1, replica_groups=mesh['day'=2,'stu'=16] {'stu'}, dimensions={1}, use_global_device_ids=true | all-gather | bytes 34816 | tf_op jit(solution)/shard_map/all_gather | solution.py:38
  419.3 0.0 collective-permute-done.7
  419.3 5.2 %multiply_reduce_fusion = (f32[]{:T(128)}, f32[32,16]{0,1:T(8,128)S(1)}) fusion(f32[32,16]{0,1:T(8,128)S(1)} %multiply_add_fusion.1, f32[7,16]{0,1:T(8,128)S(1)} %collective-permute-done.7, f32[32,16]{0,1:T(8,128)S(1)} %fusion.20, f32[]{:T(128)} %bitcast.7, f32[]{:T(128)} %bitcast.6, f32[]{:T(128)} %bitcast.5, f32[]{:T(128)} %bitcast.4, f32[]{:T(128)} %bitcast.3, ...), kind=kOutput, calls=%fused_computation.227 | convolution fusion | flops 1585151 | bytes 55776 | tf_op jit(solution)/shard_map/dot_general | solution.py:37
  424.5 32.0 %psum.102 = f32[]{:T(128)} all-reduce(f32[]{:T(128)} %get-tuple-element.8), channel_id=1, replica_groups=mesh['day'=2,'stu'=16] {'stu'}, use_global_device_ids=true, to_apply=%region_19.0 | all-reduce | flops 1 | bytes 8 | tf_op jit(solution)/shard_map/psum | solution.py:50
  456.5 6.1 %psum.103 = f32[]{:T(128)} all-reduce(f32[]{:T(128)} %psum.102), channel_id=1, replica_groups=mesh['day'=2,'stu'=16] {'day'}, use_global_device_ids=true, to_apply=%region_20.0 | all-reduce | flops 1 | bytes 8 | tf_op jit(solution)/shard_map/psum | solution.py:50
  463.9 0.6 multiply_subtract_fusion
  (6 shorter events, 0.0 us)
Async XLA Ops:
  7.2 8.3 %copy-start = (bf16[1024,256]{1,0:T(8,128)(2,1)S(1)}, bf16[1024,256]{1,0:T(8,128)(2,1)}, u32[]{:S(2)}) copy-start(bf16[1024,256]{1,0:T(8,128)(2,1)} %param.7) | copy-start | bytes 1572868
  7.2 8.3 %copy-start.1 = (bf16[32,8,1024]{2,1,0:T(8,128)(2,1)S(1)}, bf16[32,8,1024]{2,1,0:T(8,128)(2,1)}, u32[]{:S(2)}) copy-start(bf16[32,8,1024]{2,1,0:T(8,128)(2,1)} %param.5) | copy-start | bytes 1572868
  7.2 97.0 %all-reduce.4.cloned.1.call-start = ((), (), s32[]{:S(2)}) async-start(), calls=%async_computation.2 | async-start | bytes 524288 | tf_op jit(solution)/shard_map/psum | solution.py:54
  8.3 31.6 %collective-permute-start = (f32[7,16]{0,1:T(8,128)S(1)}, f32[7,16]{0,1:T(8,128)S(1)}, u32[]{:S(2)}, u32[]{:S(2)}) collective-permute-start(f32[7,16]{0,1:T(8,128)S(1)} %slice.333), channel_id=1, source_target_pairs={{0,16},{1,17},{2,18},{3,19},{4,20},{5,21},{6,22},{7,23},{8,24},{9,... | collective-permute-start | bytes 1352 | tf_op jit(solution)/shard_map/ppermute | solution.py:14
  14.8 0.7 copy-start.2
  14.8 148.3 %reduce-scatter.2.cloned.1.call-start = ((), (), s32[]{:S(2)}) async-start(), calls=%async_computation.1 | async-start | bytes 139264 | tf_op jit(solution)/shard_map/reduce_scatter | solution.py:72
  16.6 0.7 copy-start.3
  44.4 60.5 %collective-permute-start.1 = (f32[7,16]{0,1:T(8,128)S(1)}, f32[7,16]{0,1:T(8,128)S(1)}, u32[]{:S(2)}, u32[]{:S(2)}) collective-permute-start(f32[7,16]{0,1:T(8,128)S(1)} %bitcast.27), channel_id=1, source_target_pairs={{16,0},{17,1},{18,2},{19,3},{20,4},{21,5},{22,6},{23,7},{24,8},{25... | collective-permute-start | bytes 1352 | tf_op jit(solution)/shard_map/ppermute | solution.py:14
  168.5 4.7 %collective-permute-start.2 = (f32[7,16]{0,1:T(8,128)S(1)}, f32[7,16]{0,1:T(8,128)S(1)}, u32[]{:S(2)}, u32[]{:S(2)}) collective-permute-start(f32[7,16]{0,1:T(8,128)S(1)} %slice.359), channel_id=1, source_target_pairs={{0,16},{1,17},{2,18},{3,19},{4,20},{5,21},{6,22},{7,23},{8,24},{9,... | collective-permute-start | bytes 1352 | tf_op jit(solution)/shard_map/ppermute | solution.py:14
  177.7 21.1 %collective-permute-start.3 = (f32[7,16]{0,1:T(8,128)S(1)}, f32[7,16]{0,1:T(8,128)S(1)}, u32[]{:S(2)}, u32[]{:S(2)}) collective-permute-start(f32[7,16]{0,1:T(8,128)S(1)} %bitcast.29), channel_id=1, source_target_pairs={{16,0},{17,1},{18,2},{19,3},{20,4},{21,5},{22,6},{23,7},{24,8},{25... | collective-permute-start | bytes 1352 | tf_op jit(solution)/shard_map/ppermute | solution.py:14
  279.9 5.3 %collective-permute-start.4 = (f32[7,16]{0,1:T(8,128)S(1)}, f32[7,16]{0,1:T(8,128)S(1)}, u32[]{:S(2)}, u32[]{:S(2)}) collective-permute-start(f32[7,16]{0,1:T(8,128)S(1)} %slice.385), channel_id=1, source_target_pairs={{0,16},{1,17},{2,18},{3,19},{4,20},{5,21},{6,22},{7,23},{8,24},{9,... | collective-permute-start | bytes 1352 | tf_op jit(solution)/shard_map/ppermute | solution.py:14
  289.7 18.8 %collective-permute-start.5 = (f32[7,16]{0,1:T(8,128)S(1)}, f32[7,16]{0,1:T(8,128)S(1)}, u32[]{:S(2)}, u32[]{:S(2)}) collective-permute-start(f32[7,16]{0,1:T(8,128)S(1)} %bitcast.30), channel_id=1, source_target_pairs={{16,0},{17,1},{18,2},{19,3},{20,4},{21,5},{22,6},{23,7},{24,8},{25... | collective-permute-start | bytes 1352 | tf_op jit(solution)/shard_map/ppermute | solution.py:14
  390.7 5.3 %collective-permute-start.6 = (f32[7,16]{0,1:T(8,128)S(1)}, f32[7,16]{0,1:T(8,128)S(1)}, u32[]{:S(2)}, u32[]{:S(2)}) collective-permute-start(f32[7,16]{0,1:T(8,128)S(1)} %slice.411), channel_id=1, source_target_pairs={{0,16},{1,17},{2,18},{3,19},{4,20},{5,21},{6,22},{7,23},{8,24},{9,... | collective-permute-start | bytes 1352 | tf_op jit(solution)/shard_map/ppermute | solution.py:14
  400.5 18.8 %collective-permute-start.7 = (f32[7,16]{0,1:T(8,128)S(1)}, f32[7,16]{0,1:T(8,128)S(1)}, u32[]{:S(2)}, u32[]{:S(2)}) collective-permute-start(f32[7,16]{0,1:T(8,128)S(1)} %bitcast.28), channel_id=1, source_target_pairs={{16,0},{17,1},{18,2},{19,3},{20,4},{21,5},{22,6},{23,7},{24,8},{25... | collective-permute-start | bytes 1352 | tf_op jit(solution)/shard_map/ppermute | solution.py:14
Sparse Core Ops, SparseCore 0:
  15.0 89.1 all-reduce.3
  107.6 55.5 reduce-scatter.1
